TPU v7x, 32 devices: a whole 2x2x4 slice. The times are simulated.
32 devices in a mesh: tile: 8 (over y, x, core), sect: 2 (over z_hi), lev: 2 (over z_lo).
Axes of the slice: x: 2, y: 2, z: 4 (z_hi: 2, z_lo: 2; z = z_hi * 2 + z_lo), core: 2. Of those that a mesh axis runs over, the one named last changes fastest.
Arguments:
- adjoint: float32 [2, 8, 64, 128, 128], P('sect', 'tile', 'lev'), may hold values from -6 to 6
- diffusion: float32 [2, 8, 128, 128], P('sect', 'tile'), may hold values from 0.02 to 0.12
- wet_mask: int32 [2, 8, 128, 128], P('sect', 'tile'), may hold values 0 or 1
- remap: int32 [2, 8, 128], P('sect', 'tile'), may hold values from 0 to 127
- coupling: float32 [2, 64], P('sect', 'lev'), may hold values from 0.1 to 0.5
- vert_inverse: float32 [2, 8, 64, 64], P('sect', 'tile')
- nbr_tile: int32 [8, 4], P('tile'), may hold values from -1 to 7, as said below
- nbr_side: int32 [8, 4], P('tile'), may hold values from 0 to 3
- nbr_flip: int32 [8, 4], P('tile'), may hold values from 0 to 1
Outputs:
- result: float32 [2, 8, 64, 128, 128], P('sect', 'tile', 'lev')
Inputs may be any that keep to these rules, and one draw needn't show every extreme that they name: `nbr_tile`: A side with a neighbour is named back by that neighbour's named side with the same flip.
All inputs are finite; a program needn't handle non-finite values. No bound on the sum of `wet_mask` on one device may be relied on, other than what follows from the above.
Results may differ from a plain program's by a relative error of at most 0.0001.
Values sent between devices are 32-bit elements; how exact they have to be, the bound alone decides.
No kernel may reach another device: no remote copies, remote signals or barrier semaphores. Data moves between devices by JAX's collectives and lax.ppermute only.
A program may use at most 64 MiB of HBM per device.

v0:
```python
import jax
import jax.numpy as jnp
from jax import lax
from jax.sharding import PartitionSpec as P


def swapped(block, axis, bit):
    count = lax.axis_size(axis)
    route = []
    for low in range(count):
        high = low | 1 << bit
        if high != low and high < count:
            route += [(low, high), (high, low)]
    return lax.ppermute(block, axis, route)


def edge_rows(field):
    return jnp.stack(
        [field[..., 0, :], field[..., -1, :], field[..., :, 0], field[..., :, -1]], axis=-3
    )


def oriented(picked, flips):
    return jnp.where((flips == 1)[:, :, None, None], picked[..., ::-1], picked)


def laplace(field, halo):
    side_cells = field.shape[3]
    position = lax.broadcasted_iota(jnp.int32, (1, 1, 1, side_cells), 3)
    upper = jnp.concatenate([halo[:, 0][:, :, None, :], field[:, :, :-1, :]], axis=2)
    lower = jnp.concatenate([field[:, :, 1:, :], halo[:, 1][:, :, None, :]], axis=2)
    left_side = jnp.pad(field[:, :, :, :-1], ((0, 0), (0, 0), (0, 0), (1, 0)))
    left_side = left_side + jnp.where(position == 0, halo[:, 2][:, :, :, None], jnp.float32(0.0))
    right_side = jnp.pad(field[:, :, :, 1:], ((0, 0), (0, 0), (0, 0), (0, 1)))
    right_side = right_side + jnp.where(
        position == side_cells - 1, halo[:, 3][:, :, :, None], jnp.float32(0.0)
    )
    return upper + lower + left_side + right_side - 4.0 * field


def pick_tile_rows(field, rows):
    return field[:, rows, :]


def on_device(
    adjoint, diffusion, wet_mask, remap, coupling, vert_inverse, nbr_tile, nbr_side, nbr_flip
):
    current = adjoint[0]
    diffusivity = diffusion[0]
    wet_cells = wet_mask[0].astype(jnp.float32)
    remap_rows = remap[0]
    level_gain = coupling[0]
    inverse = vert_inverse[0]
    level_rows = current.shape[1]
    my_first = lax.axis_index("lev") * level_rows
    for step in range(2):
        partner = swapped(current, "sect", 0)
        pulled = jax.vmap(pick_tile_rows)(partner, remap_rows)
        coupled = current + level_gain[None, :, None, None] * pulled
        whole = lax.all_gather(coupled, "lev", axis=1, tiled=True)
        own_columns = lax.dynamic_slice_in_dim(inverse, my_first, level_rows, 2)
        column = jnp.einsum("tkl,tkxy->tlxy", own_columns, whole, precision=lax.Precision.HIGHEST)
        flux = wet_cells[:, None] * diffusivity[:, None] * column
        edges = edge_rows(flux)
        all_edges = lax.all_gather(edges, "tile", axis=0, tiled=True)
        picked = all_edges[jnp.maximum(nbr_tile, 0), nbr_side]
        halo = jnp.where(
            (nbr_tile >= 0)[:, :, None, None], oriented(picked, nbr_flip), jnp.float32(0.0)
        )
        current = wet_cells[:, None] * (column + laplace(flux, halo))
    return current[None]


def solution(mesh):
    in_specs = (
        P("sect", "tile", "lev", None, None),
        P("sect", "tile", None, None),
        P("sect", "tile", None, None),
        P("sect", "tile", None),
        P("sect", "lev"),
        P("sect", "tile", None, None),
        P("tile", None),
        P("tile", None),
        P("tile", None),
    )
    out_specs = P("sect", "tile", "lev", None, None)
    return jax.shard_map(
        on_device, mesh=mesh, in_specs=in_specs, out_specs=out_specs, check_vma=False
    )
```

profile of v0, /device:TPU:0, one launch (start us, length us, event | category | flops | bytes accessed | tf_op | source)
XLA Modules:
  0.0 405.9 jit_solution(2878523833001333384)
XLA Ops:
  6.5 2.8 copy.65
  9.4 4.1 %collective-permute-start = (f32[1,32,128,128]{3,1,2,0:T(8,128)S(1)}, f32[1,32,128,128]{3,1,2,0:T(8,128)}, u32[]{:S(2)}, u32[]{:S(2)}) collective-permute-start(f32[1,32,128,128]{3,1,2,0:T(8,128)S(1)} %bitcast.109), channel_id=1, source_target_pairs={{0,2},{2,0},{1,3},{3,1},{4,6},{6,4},{5,7},{7,5},{8,10},{10,8},{9,1... | collective-permute-start | bytes 6291464 | tf_op jit(solution)/shard_map/ppermute | solution.py:14
  13.5 90.6 %collective-permute-done = f32[1,32,128,128]{3,1,2,0:T(8,128)} collective-permute-done((f32[1,32,128,128]{3,1,2,0:T(8,128)S(1)}, f32[1,32,128,128]{3,1,2,0:T(8,128)}, u32[]{:S(2)}, u32[]{:S(2)}) %collective-permute-start) | collective-permute-done | bytes 2097184 | tf_op jit(solution)/shard_map/ppermute | solution.py:14
  104.1 3.6 gather_fusion.2
  107.8 4.2 %fusion.16 = f32[1,32,128,128]{3,1,2,0:T(8,128)} fusion(f32[128,32,128]{2,1,0:T(8,128)} %gather_fusion.2, f32[32]{0:T(128)S(1)} %bitcast.114, f32[1,1,32,128,128]{4,3,2,1,0:T(8,128)S(1)} %copy-done.3), kind=kLoop, calls=%fused_computation.24 | loop fusion | flops 1048576 | bytes 6291584 | tf_op jit(solution)/shard_map/add | solution.py:59
  112.1 0.5 copy-done.7
  112.9 57.2 %all-gather.3.cloned.1.call-done = f32[1,64,128,128]{3,1,2,0:T(8,128)} async-done(((f32[1,32,128,128]{3,1,2,0:T(8,128)}), f32[1,64,128,128]{3,1,2,0:T(8,128)}) %all-gather.3.cloned.1.call-update) | async-done | bytes 4194320 | tf_op jit(solution)/shard_map/all_gather | solution.py:60
  170.1 4.0 fusion.2
  174.5 2.7 fusion.30
  177.2 2.8 fusion.31
  180.0 2.7 fusion.29
  182.7 2.7 copy.54
  185.3 2.7 copy.53
  188.0 10.0 %all_gather.13 = f32[8,4,32,128]{3,2,1,0:T(8,128)S(1)} all-gather(f32[1,4,32,128]{3,2,1,0:T(8,128)S(1)} %pad_maximum_fusion), channel_id=1, replica_groups=mesh['tile'=8,'sect'=2,'lev'=2] {'tile'}, dimensions={0}, use_global_device_ids=true | all-gather | bytes 589824 | tf_op jit(solution)/shard_map/all_gather | solution.py:65
  198.0 0.6 gather_fusion
  199.0 5.3 %fusion.8 = f32[1,32,128,128]{3,1,2,0:T(8,128)S(1)} fusion(f32[1,32,127,128]{3,1,2,0:T(8,128)} %get-tuple-element.16, f32[1,32,1,128]{3,1,2,0:T(8,128)S(1)} %get-tuple-element.28, f32[1,32,1,128]{3,1,2,0:T(8,128)S(1)} %get-tuple-element.27, f32[1,32,127,128]{3,1,2,0:T(8,128)} %get-tuple-element.15, f32[32,128,128]{2,0,1:T(8,128)S(1)} %fusion.2, ...), kind=kLoop, calls=%fused_computation.13 | loop fusion | flops 7340032 | bytes 12714240 | tf_op jit(solution)/shard_map/mul | solution.py:70
  204.3 1.3 copy-done.1
  205.6 2.4 collective-permute-start.1
  208.0 91.4 %collective-permute-done.1 = f32[1,32,128,128]{3,1,2,0:T(8,128)} collective-permute-done((f32[1,32,128,128]{3,1,2,0:T(8,128)S(1)}, f32[1,32,128,128]{3,1,2,0:T(8,128)}, u32[]{:S(2)}, u32[]{:S(2)}) %collective-permute-start.1) | collective-permute-done | bytes 2097184 | tf_op jit(solution)/shard_map/ppermute | solution.py:14
  299.4 3.6 gather_fusion.3
  303.0 3.5 fusion.15
  306.5 56.0 %all-gather.5.cloned.1.call-done = f32[1,64,128,128]{3,1,2,0:T(8,128)} async-done(((f32[1,32,128,128]{3,1,2,0:T(8,128)}), f32[1,64,128,128]{3,1,2,0:T(8,128)}) %all-gather.5.cloned.1.call-update) | async-done | bytes 4194320 | tf_op jit(solution)/shard_map/all_gather | solution.py:60
  362.5 4.0 fusion
  366.9 2.7 fusion.27
  369.6 2.8 fusion.28
  372.3 2.7 fusion.26
  375.1 2.7 copy.58
  377.7 2.7 copy.57
  380.4 9.8 %all_gather.15 = f32[8,4,32,128]{3,2,1,0:T(8,128)S(1)} all-gather(f32[1,4,32,128]{3,2,1,0:T(8,128)S(1)} %pad_maximum_fusion.1), channel_id=1, replica_groups=mesh['tile'=8,'sect'=2,'lev'=2] {'tile'}, dimensions={0}, use_global_device_ids=true | all-gather | bytes 589824 | tf_op jit(solution)/shard_map/all_gather | solution.py:65
  390.2 0.6 gather_fusion.1
  391.1 5.3 %fusion.14 = f32[1,1,32,128,128]{4,2,3,1,0:T(8,128)S(1)} fusion(f32[1,32,127,128]{3,1,2,0:T(8,128)} %get-tuple-element.8, f32[1,32,1,128]{3,1,2,0:T(8,128)S(1)} %get-tuple-element.24, f32[1,32,1,128]{3,1,2,0:T(8,128)S(1)} %get-tuple-element.23, f32[1,32,127,128]{3,1,2,0:T(8,128)} %get-tuple-element.7, f32[32,128,128]{2,0,1:T(8,128)S(1)} %fusion, ...), kind=kLoop, calls=%fused_computation.20 | loop fusion | flops 7340032 | bytes 12714240 | tf_op jit(solution)/shard_map/broadcast_in_dim | solution.py:71
  396.5 2.5 copy.61
  (50 shorter events, 1.8 us)
Async XLA Ops:
  6.5 163.6 %copy-start = (f32[1,1,64,64]{3,2,1,0:T(8,128)S(1)}, f32[1,1,64,64]{3,2,1,0:T(8,128)}, u32[]{:S(2)}) copy-start(f32[1,1,64,64]{3,2,1,0:T(8,128)} %param.14) | copy-start | bytes 49156
  6.5 6.9 %copy-start.10 = (s32[1,1,128]{2,1,0:T(1,128)S(1)}, s32[1,1,128]{2,1,0:T(1,128)}, u32[]{:S(2)}) copy-start(s32[1,1,128]{2,1,0:T(1,128)} %param.12) | copy-start | bytes 1540
  6.5 163.6 %all-gather.3.cloned.1.call-start = ((), (), s32[]{:S(2)}) async-start(), calls=%async_computation | async-start | bytes 6291456 | tf_op jit(solution)/shard_map/all_gather | solution.py:60
  9.4 94.8 %collective-permute-start = (f32[1,32,128,128]{3,1,2,0:T(8,128)S(1)}, f32[1,32,128,128]{3,1,2,0:T(8,128)}, u32[]{:S(2)}, u32[]{:S(2)}) collective-permute-start(f32[1,32,128,128]{3,1,2,0:T(8,128)S(1)} %bitcast.109), channel_id=1, source_target_pairs={{0,2},{2,0},{1,3},{3,1},{4,6},{6,4},{5,7},{7,5},{8,10},{10,8},{9,1... | collective-permute-start | bytes 6291464 | tf_op jit(solution)/shard_map/ppermute | solution.py:14
  13.5 94.2 %copy-start.3 = (f32[1,1,32,128,128]{4,3,2,1,0:T(8,128)S(1)}, f32[1,1,32,128,128]{4,3,2,1,0:T(8,128)}, u32[]{:S(2)}) copy-start(f32[1,1,32,128,128]{4,3,2,1,0:T(8,128)} %param.9) | copy-start | bytes 6291460
  13.5 94.2 %copy-start.6 = (f32[1,32]{1,0:T(1,128)S(1)}, f32[1,32]{1,0:T(1,128)}, u32[]{:S(2)}) copy-start(f32[1,32]{1,0:T(1,128)} %param.13) | copy-start | bytes 388
  112.0 0.7 copy-start.7
  112.0 0.7 copy-start.8
  112.0 0.7 copy-start.9
  112.0 0.9 copy-start.4
  112.0 0.9 copy-start.5
  112.0 250.5 %all-gather.5.cloned.1.call-start = ((), (), s32[]{:S(2)}) async-start(), calls=%async_computation.1 | async-start | bytes 6291456 | tf_op jit(solution)/shard_map/all_gather | solution.py:60
  204.3 1.3 copy-start.1
  205.6 93.8 %collective-permute-start.1 = (f32[1,32,128,128]{3,1,2,0:T(8,128)S(1)}, f32[1,32,128,128]{3,1,2,0:T(8,128)}, u32[]{:S(2)}, u32[]{:S(2)}) collective-permute-start(f32[1,32,128,128]{3,1,2,0:T(8,128)S(1)} %fusion.8), channel_id=1, source_target_pairs={{0,2},{2,0},{1,3},{3,1},{4,6},{6,4},{5,7},{7,5},{8,10},{10,8},{9,1... | collective-permute-start | bytes 6291464 | tf_op jit(solution)/shard_map/ppermute | solution.py:14
  208.0 95.0 %copy-start.2 = (f32[1,32,128,128]{3,1,2,0:T(8,128)S(1)}, f32[1,32,128,128]{3,1,2,0:T(8,128)}, u32[]{:S(2)}) copy-start(f32[1,32,128,128]{3,1,2,0:T(8,128)} %copy-done.1) | copy-start | bytes 6291460
Sparse Core Ops, SparseCore 0:
  112.2 57.9 all-gather.2
  306.6 55.8 all-gather.4
where the time goes:
time: 406 us
  waiting for transfers between devices  295 us (73%)
  local copies, waits for them, and re-layouts  43.3 us (11%)
  blocking collectives  19.8 us (5%)
  other arithmetic  19.3 us (5%)
  between operations  13.6 us (3%)
  matrix products  8 us (2%)
  starting transfers between devices  6.55 us (2%)
    ppermute x2, waiting for transfers between devices, swapped(): return lax.ppermute(block, axis, route)  182 us
    all_gather x2, waiting for transfers between devices, on_device(): whole = lax.all_gather(coupled, 'lev', axis=1, tiled=True)  113 us
    all_gather x2, blocking collectives, on_device(): all_edges = lax.all_gather(edges, 'tile', axis=0, tiled=True)  19.8 us
    slice x4, local copies, waits for them, and re-layouts, edge_rows(): field[..., :, 0]  10.8 us
  transfers between devices with their start and end apart: 4, of which 4 were waited for; matrix products, arithmetic and copies ran while one was open for 0% of the time, Pallas kernels for 0%

commit v1 on v0

--- a/solution.py
+++ b/solution.py
@@ -2,6 +2,7 @@
 import jax.numpy as jnp
 from jax import lax
 from jax.sharding import PartitionSpec as P
+from jax.lax import axis_index, ppermute, psum
 
 
 def swapped(block, axis, bit):
@@ -62,7 +63,20 @@
         column = jnp.einsum("tkl,tkxy->tlxy", own_columns, whole, precision=lax.Precision.HIGHEST)
         flux = wet_cells[:, None] * diffusivity[:, None] * column
         edges = edge_rows(flux)
-        all_edges = lax.all_gather(edges, "tile", axis=0, tiled=True)
+        outer, y2, arr_out = (psum(1, "tile"), axis_index("tile"), edges.shape[0])
+        frame_out, k_now = (edges, 1)
+        while k_now < outer:
+            frame_out = jnp.concatenate(
+                [
+                    frame_out,
+                    ppermute(
+                        frame_out, "tile", [(at, (at - k_now) % outer) for at in range(outer)]
+                    ),
+                ],
+                axis=0,
+            )
+            k_now = 2 * k_now
+        all_edges = jnp.roll(frame_out, shift=y2 * arr_out, axis=0)
         picked = all_edges[jnp.maximum(nbr_tile, 0), nbr_side]
         halo = jnp.where(
             (nbr_tile >= 0)[:, :, None, None], oriented(picked, nbr_flip), jnp.float32(0.0)

time: 406 us -> 414 us (1.020)
  blocking collectives: 19.8 us -> 0 us
  waiting for transfers between devices: 295 us -> 313 us
  starting transfers between devices: 6.55 us -> 13.5 us
    all_gather x2 -> x0, blocking collectives: 19.8 us -> none  [on_device(): all_edges = lax.all_gather(edges, 'tile', axis=0, tiled=True)]
    ppermute x0 -> x6, waiting for transfers between devices: none -> 17.8 us  [on_device(): ppermute(frame_out, 'tile', [(at, (at - k_now) % outer) for at in range(o...]
    ppermute x0 -> x6, starting transfers between devices: none -> 6.87 us  [on_device(): ppermute(frame_out, 'tile', [(at, (at - k_now) % outer) for at in range(o...]
    slice x2 -> x4, local copies, waits for them, and re-layouts: 5.31 us -> 10.8 us  [edge_rows(): field[..., :, -1]]
    slice x4 -> x2, local copies, waits for them, and re-layouts: 10.8 us -> 5.31 us  [edge_rows(): field[..., :, 0]]
  transfers between devices with their start and end apart: 4 -> 10, of which waited for: 4 -> 10; matrix products, arithmetic and copies ran while one was open for 0% -> 3% of each run, Pallas kernels for 0% -> 0%
where the time goes in v1:
time: 414 us; the launch traced here: 413 us
  waiting for transfers between devices  313 us (76%)
  local copies, waits for them, and re-layouts  43.9 us (11%)
  other arithmetic  21 us (5%)
  between operations  13.6 us (3%)
  starting transfers between devices  13.5 us (3%)
  matrix products  7.99 us (2%)
    ppermute x2, waiting for transfers between devices, swapped(): return lax.ppermute(block, axis, route)  181 us
    all_gather x2, waiting for transfers between devices, on_device(): whole = lax.all_gather(coupled, 'lev', axis=1, tiled=True)  115 us
    ppermute x6, waiting for transfers between devices, on_device(): ppermute(frame_out, 'tile', [(at, (at - k_now) % outer) for at in range(o...  17.8 us
    slice x4, local copies, waits for them, and re-layouts, edge_rows(): field[..., :, -1]  10.8 us
  transfers between devices with their start and end apart: 10, of which 10 were waited for; matrix products, arithmetic and copies ran while one was open for 3% of the time, Pallas kernels for 0%

profile of v1, /device:TPU:0, one launch (start us, length us, event | category | flops | bytes accessed | tf_op | source)
XLA Modules:
  0.0 413.0 jit_solution(12528891724749206213)
XLA Ops:
  6.5 2.8 copy.54
  9.4 4.1 collective-permute-start
  13.5 90.6 %collective-permute-done = f32[1,32,128,128]{3,1,2,0:T(8,128)} collective-permute-done((f32[1,32,128,128]{3,1,2,0:T(8,128)S(1)}, f32[1,32,128,128]{3,1,2,0:T(8,128)}, u32[]{:S(2)}, u32[]{:S(2)}) %collective-permute-start) | collective-permute-done | bytes 2097184 | tf_op jit(solution)/shard_map/ppermute | solution.py:15
  104.1 3.6 gather_fusion.2
  107.8 4.2 %fusion.16 = f32[1,32,128,128]{3,1,2,0:T(8,128)} fusion(f32[128,32,128]{2,1,0:T(8,128)} %gather_fusion.2, f32[32]{0:T(128)S(1)} %bitcast.126, f32[1,1,32,128,128]{4,3,2,1,0:T(8,128)S(1)} %copy-done.3), kind=kLoop, calls=%fused_computation.24 | loop fusion | flops 1048576 | bytes 6291584 | tf_op jit(solution)/shard_map/add | solution.py:60
  112.9 57.2 %all-gather.3.cloned.1.call-done = f32[1,64,128,128]{3,1,2,0:T(8,128)} async-done(((f32[1,32,128,128]{3,1,2,0:T(8,128)}), f32[1,64,128,128]{3,1,2,0:T(8,128)}) %all-gather.3.cloned.1.call-update) | async-done | bytes 4194320 | tf_op jit(solution)/shard_map/all_gather | solution.py:61
  170.1 4.0 fusion.2
  175.5 2.8 fusion.57
  178.3 2.7 copy.42
  180.9 2.7 copy.43
  185.5 1.9 collective-permute-done.1
  188.2 2.8 fusion.55
  190.9 2.5 collective-permute-done.2
  194.3 2.6 fusion.56
  197.0 4.5 %collective-permute-done.3 = f32[4,4,32,128]{3,2,1,0:T(8,128)S(1)} collective-permute-done((f32[4,4,32,128]{3,2,1,0:T(8,128)S(1)}, f32[4,4,32,128]{3,2,1,0:T(8,128)S(1)}, u32[]{:S(2)}, u32[]{:S(2)}) %collective-permute-start.3) | collective-permute-done | bytes 262176 | tf_op jit(solution)/shard_map/ppermute | solution.py:72
  202.9 5.7 %fusion.8 = f32[1,32,128,128]{3,1,2,0:T(8,128)S(1)} fusion(f32[1,32,127,128]{3,1,2,0:T(8,128)} %get-tuple-element.17, f32[1,32,1,128]{3,1,2,0:T(8,128)S(1)} %get-tuple-element.29, f32[1,32,1,128]{3,1,2,0:T(8,128)S(1)} %get-tuple-element.28, f32[1,32,127,128]{3,1,2,0:T(8,128)} %get-tuple-element.16, f32[32,128,128]{2,0,1:T(8,128)} %copy-done.2, ...), kind=kLoop, calls=%fused_computation.13 | loop fusion | flops 7340032 | bytes 12714240 | tf_op jit(solution)/shard_map/mul | solution.py:84
  208.6 2.5 collective-permute-start.4
  211.1 89.9 %collective-permute-done.4 = f32[1,32,128,128]{3,1,2,0:T(8,128)} collective-permute-done((f32[1,32,128,128]{3,1,2,0:T(8,128)S(1)}, f32[1,32,128,128]{3,1,2,0:T(8,128)}, u32[]{:S(2)}, u32[]{:S(2)}) %collective-permute-start.4) | collective-permute-done | bytes 2097184 | tf_op jit(solution)/shard_map/ppermute | solution.py:15
  300.9 3.6 gather_fusion.3
  304.5 3.5 fusion.15
  308.0 57.4 %all-gather.5.cloned.1.call-done = f32[1,64,128,128]{3,1,2,0:T(8,128)} async-done(((f32[1,32,128,128]{3,1,2,0:T(8,128)}), f32[1,64,128,128]{3,1,2,0:T(8,128)}) %all-gather.5.cloned.1.call-update) | async-done | bytes 4194320 | tf_op jit(solution)/shard_map/all_gather | solution.py:61
  365.4 4.0 fusion
  370.8 2.8 fusion.54
  373.5 2.7 copy.46
  376.2 2.7 copy.47
  380.7 1.9 collective-permute-done.5
  383.3 2.8 fusion.52
  386.0 2.5 collective-permute-done.6
  389.4 2.6 fusion.53
  392.0 4.5 %collective-permute-done.7 = f32[4,4,32,128]{3,2,1,0:T(8,128)S(1)} collective-permute-done((f32[4,4,32,128]{3,2,1,0:T(8,128)S(1)}, f32[4,4,32,128]{3,2,1,0:T(8,128)S(1)}, u32[]{:S(2)}, u32[]{:S(2)}) %collective-permute-start.7) | collective-permute-done | bytes 262176 | tf_op jit(solution)/shard_map/ppermute | solution.py:72
  397.9 5.7 %fusion.14 = f32[1,1,32,128,128]{4,2,3,1,0:T(8,128)S(1)} fusion(f32[1,32,127,128]{3,1,2,0:T(8,128)} %get-tuple-element.9, f32[1,32,1,128]{3,1,2,0:T(8,128)S(1)} %get-tuple-element.25, f32[1,32,1,128]{3,1,2,0:T(8,128)S(1)} %get-tuple-element.24, f32[1,32,127,128]{3,1,2,0:T(8,128)} %get-tuple-element.8, f32[32,128,128]{2,0,1:T(8,128)} %copy-done.1, ...), kind=kLoop, calls=%fused_computation.20 | loop fusion | flops 7340032 | bytes 12714240 | tf_op jit(solution)/shard_map/broadcast_in_dim | solution.py:85
  403.7 2.5 copy.50
  (66 shorter events, 13.3 us)
Async XLA Ops:
  6.5 163.6 %copy-start = (f32[1,1,64,64]{3,2,1,0:T(8,128)S(1)}, f32[1,1,64,64]{3,2,1,0:T(8,128)}, u32[]{:S(2)}) copy-start(f32[1,1,64,64]{3,2,1,0:T(8,128)} %param.16) | copy-start | bytes 49156
  6.5 6.9 %copy-start.10 = (s32[1,1,128]{2,1,0:T(1,128)S(1)}, s32[1,1,128]{2,1,0:T(1,128)}, u32[]{:S(2)}) copy-start(s32[1,1,128]{2,1,0:T(1,128)} %param.14) | copy-start | bytes 1540
  6.5 163.6 %all-gather.3.cloned.1.call-start = ((), (), s32[]{:S(2)}) async-start(), calls=%async_computation | async-start | bytes 6291456 | tf_op jit(solution)/shard_map/all_gather | solution.py:61
  9.4 94.8 %collective-permute-start = (f32[1,32,128,128]{3,1,2,0:T(8,128)S(1)}, f32[1,32,128,128]{3,1,2,0:T(8,128)}, u32[]{:S(2)}, u32[]{:S(2)}) collective-permute-start(f32[1,32,128,128]{3,1,2,0:T(8,128)S(1)} %bitcast.109), channel_id=1, source_target_pairs={{0,2},{2,0},{1,3},{3,1},{4,6},{6,4},{5,7},{7,5},{8,10},{10,8},{9,1... | collective-permute-start | bytes 6291464 | tf_op jit(solution)/shard_map/ppermute | solution.py:15
  13.5 94.2 %copy-start.3 = (f32[1,1,32,128,128]{4,3,2,1,0:T(8,128)S(1)}, f32[1,1,32,128,128]{4,3,2,1,0:T(8,128)}, u32[]{:S(2)}) copy-start(f32[1,1,32,128,128]{4,3,2,1,0:T(8,128)} %param.11) | copy-start | bytes 6291460
  13.5 94.2 %copy-start.6 = (f32[1,32]{1,0:T(1,128)S(1)}, f32[1,32]{1,0:T(1,128)}, u32[]{:S(2)}) copy-start(f32[1,32]{1,0:T(1,128)} %param.15) | copy-start | bytes 388
  112.0 0.7 copy-start.7
  112.0 0.7 copy-start.8
  112.0 0.7 copy-start.9
  112.0 0.9 copy-start.4
  112.0 0.9 copy-start.5
  112.0 253.4 %all-gather.5.cloned.1.call-start = ((), (), s32[]{:S(2)}) async-start(), calls=%async_computation.1 | async-start | bytes 6291456 | tf_op jit(solution)/shard_map/all_gather | solution.py:61
  174.1 1.4 copy-start.2
  183.6 3.8 collective-permute-start.1
  187.4 6.1 %collective-permute-start.2 = (f32[2,4,32,128]{3,2,1,0:T(8,128)S(1)}, f32[2,4,32,128]{3,2,1,0:T(8,128)S(1)}, u32[]{:S(2)}, u32[]{:S(2)}) collective-permute-start(f32[2,4,32,128]{3,2,1,0:T(8,128)S(1)} %pad_maximum_fusion.2), channel_id=1, source_target_pairs={{0,24},{4,28},{8,0},{12,4},{16,8},{20,12},{24,16},{28,20},{1,25},{... | collective-permute-start | bytes 393224 | tf_op jit(solution)/shard_map/ppermute | solution.py:72
  193.5 8.0 %collective-permute-start.3 = (f32[4,4,32,128]{3,2,1,0:T(8,128)S(1)}, f32[4,4,32,128]{3,2,1,0:T(8,128)S(1)}, u32[]{:S(2)}, u32[]{:S(2)}) collective-permute-start(f32[4,4,32,128]{3,2,1,0:T(8,128)S(1)} %pad_maximum_fusion), channel_id=1, source_target_pairs={{0,16},{4,20},{8,24},{12,28},{16,0},{20,4},{24,8},{28,12},{1,17},{... | collective-permute-start | bytes 786440 | tf_op jit(solution)/shard_map/ppermute | solution.py:72
  208.6 92.4 %collective-permute-start.4 = (f32[1,32,128,128]{3,1,2,0:T(8,128)S(1)}, f32[1,32,128,128]{3,1,2,0:T(8,128)}, u32[]{:S(2)}, u32[]{:S(2)}) collective-permute-start(f32[1,32,128,128]{3,1,2,0:T(8,128)S(1)} %fusion.8), channel_id=1, source_target_pairs={{0,2},{2,0},{1,3},{3,1},{4,6},{6,4},{5,7},{7,5},{8,10},{10,8},{9,1... | collective-permute-start | bytes 6291464 | tf_op jit(solution)/shard_map/ppermute | solution.py:15
  369.4 1.4 copy-start.1
  378.8 3.8 collective-permute-start.5
  382.6 5.9 %collective-permute-start.6 = (f32[2,4,32,128]{3,2,1,0:T(8,128)S(1)}, f32[2,4,32,128]{3,2,1,0:T(8,128)S(1)}, u32[]{:S(2)}, u32[]{:S(2)}) collective-permute-start(f32[2,4,32,128]{3,2,1,0:T(8,128)S(1)} %pad_maximum_fusion.3), channel_id=1, source_target_pairs={{0,24},{4,28},{8,0},{12,4},{16,8},{20,12},{24,16},{28,20},{1,25},{... | collective-permute-start | bytes 393224 | tf_op jit(solution)/shard_map/ppermute | solution.py:72
  388.5 8.0 %collective-permute-start.7 = (f32[4,4,32,128]{3,2,1,0:T(8,128)S(1)}, f32[4,4,32,128]{3,2,1,0:T(8,128)S(1)}, u32[]{:S(2)}, u32[]{:S(2)}) collective-permute-start(f32[4,4,32,128]{3,2,1,0:T(8,128)S(1)} %pad_maximum_fusion.1), channel_id=1, source_target_pairs={{0,16},{4,20},{8,24},{12,28},{16,0},{20,4},{24,8},{28,12},{1,17},{... | collective-permute-start | bytes 786440 | tf_op jit(solution)/shard_map/ppermute | solution.py:72
Sparse Core Ops, SparseCore 0:
  112.2 57.9 all-gather.2
  308.2 57.1 all-gather.4
